TPU v7x, 128 devices: a whole 4x4x4 slice. The times are simulated.
128 devices in a mesh: fsdp: 32 (over x, y, core), tensor: 4 (over z).
Axes of the slice: x: 4, y: 4, z: 4, core: 2. Of those that a mesh axis runs over, the one named last changes fastest.
Arguments:
- tokens: bfloat16 [4096, 4096], P(('fsdp', 'tensor')), may hold values from -6 to 6
- gate_blocks: bfloat16 [4, 544, 128, 128], P('tensor', 'fsdp'), may hold values from -0.125 to 0.125
- gate_index: int32 [4, 544], P('tensor', 'fsdp'), may hold values from 0 to 896, as said below
- up_blocks: bfloat16 [4, 544, 128, 128], P('tensor', 'fsdp'), may hold values from -0.125 to 0.125
- up_index: int32 [4, 544], P('tensor', 'fsdp'), may hold values from 0 to 896, as said below
- d_hidden: bfloat16 [4096, 14336], P('fsdp', 'tensor'), may hold values from -6 to 6
Outputs:
- hidden: bfloat16 [4096, 14336], P('fsdp', 'tensor')
- d_tokens: bfloat16 [4096, 4096], P(('fsdp', 'tensor'))
Inputs may be any that keep to these rules, and one draw needn't show every extreme that they name: `gate_index`: row t, slots f * 17 to (f + 1) * 17 - 1 belong to fsdp index f: its live slots come first and hold distinct values r * 28 + c with r among row blocks f * 1 to (f + 1) - 1; the remaining slots hold 896. Each such shard has 11 to 17 live slots, both reached in every row; shards 2i and 2i + 1 together hold exactly 28 live slots. `up_index`: as for gate_index, drawn independently.
All inputs are finite; a program needn't handle non-finite values.
Results may differ from a plain program's by a relative error of at most 0.005.
Values may be sent and summed in bfloat16 or wider, within the bound.
No kernel may reach another device: no remote copies, remote signals or barrier semaphores. Data moves between devices by JAX's collectives and lax.ppermute only.
A program may use at most 128 MiB of HBM per device.

v0:
```python
import jax
import jax.numpy as jnp
from jax import lax
from jax.sharding import PartitionSpec as P


def positions(block_index, row_blocks, col_blocks):
    valid = block_index < row_blocks * col_blocks
    row_of = jnp.minimum(block_index // col_blocks, row_blocks - 1)
    col_of = block_index % col_blocks
    row_target = jnp.where(valid, row_of, row_blocks)
    col_target = jnp.where(valid, col_of, col_blocks)
    return (row_of, col_of, row_target, col_target)


def forward_group(total, rows_split, blocks, block_index, row_blocks, col_blocks):
    row_of, col_of, row_target, col_target = positions(block_index, row_blocks, col_blocks)
    picked = jnp.take(rows_split, row_of, axis=1)
    product = jnp.einsum("tsk,skn->tsn", picked, blocks, preferred_element_type=jnp.float32)
    return total.at[:, col_target].add(product, mode="drop")


def backward_group(total, grad_split, blocks, block_index, row_blocks, col_blocks):
    row_of, col_of, row_target, col_target = positions(block_index, row_blocks, col_blocks)
    chosen = jnp.take(grad_split, col_of, axis=1)
    product = jnp.einsum("tsn,skn->tsk", chosen, blocks, preferred_element_type=jnp.float32)
    return total.at[:, row_target].add(product, mode="drop")


def shards(tokens, gate_blocks, gate_index, up_blocks, up_index, d_hidden):
    block = gate_blocks.shape[-1]
    gathered_rows = lax.all_gather(tokens, "tensor", axis=0, tiled=True)
    row_count = gathered_rows.shape[0]
    model_width = gathered_rows.shape[1]
    row_blocks = model_width // block
    local_units = d_hidden.shape[1]
    col_blocks = local_units // block
    shard_count = lax.axis_size("fsdp")
    own_gate, own_gate_index = (gate_blocks[0], gate_index[0])
    own_up, own_up_index = (up_blocks[0], up_index[0])
    all_gate, all_gate_index, all_up, all_up_index = (
        lax.all_gather(own_gate, "fsdp", axis=0, tiled=True),
        lax.all_gather(own_gate_index, "fsdp", axis=0, tiled=True),
        lax.all_gather(own_up, "fsdp", axis=0, tiled=True),
        lax.all_gather(own_up_index, "fsdp", axis=0, tiled=True),
    )
    per_shard = own_gate.shape[0]
    group_shards = 4
    group_count = shard_count // group_shards
    group_slots = group_shards * per_shard
    grouped = (
        all_gate.reshape(group_count, group_slots, block, block),
        all_gate_index.reshape(group_count, group_slots),
        all_up.reshape(group_count, group_slots, block, block),
        all_up_index.reshape(group_count, group_slots),
    )
    rows_split = gathered_rows.reshape(row_count, row_blocks, block)

    def forward_step(carry, pieces):
        gate_acc, up_acc = carry
        gate_acc = forward_group(gate_acc, rows_split, pieces[0], pieces[1], row_blocks, col_blocks)
        up_acc = forward_group(up_acc, rows_split, pieces[2], pieces[3], row_blocks, col_blocks)
        return ((gate_acc, up_acc), None)

    empty_cols = jnp.zeros((row_count, col_blocks, block), jnp.float32)
    (gate, up), _ = lax.scan(forward_step, (empty_cols, empty_cols), grouped)
    gate = gate.reshape(row_count, local_units)
    up = up.reshape(row_count, local_units)
    sig = jax.nn.sigmoid(gate)
    active = gate * sig
    hidden = (active * up).astype(jnp.bfloat16)
    d_slice = d_hidden.astype(jnp.float32)
    d_gate = (
        (d_slice * up * sig * (1.0 + gate * (1.0 - sig)))
        .astype(jnp.bfloat16)
        .reshape(row_count, col_blocks, block)
    )
    d_up = (d_slice * active).astype(jnp.bfloat16).reshape(row_count, col_blocks, block)

    def backward_step(total, pieces):
        total = backward_group(total, d_gate, pieces[0], pieces[1], row_blocks, col_blocks)
        total = backward_group(total, d_up, pieces[2], pieces[3], row_blocks, col_blocks)
        return (total, None)

    empty_rows = jnp.zeros((row_count, row_blocks, block), jnp.float32)
    partial_grad, _ = lax.scan(backward_step, empty_rows, grouped)
    partial_grad = partial_grad.reshape(row_count, model_width)
    d_tokens = lax.psum_scatter(partial_grad, "tensor", scatter_dimension=0, tiled=True).astype(
        jnp.bfloat16
    )
    return (hidden, d_tokens)


def solution(mesh):
    in_specs = (
        P(("fsdp", "tensor"), None),
        P("tensor", "fsdp", None, None),
        P("tensor", "fsdp"),
        P("tensor", "fsdp", None, None),
        P("tensor", "fsdp"),
        P("fsdp", "tensor"),
    )
    out_specs = (P("fsdp", "tensor"), P(("fsdp", "tensor"), None))
    return jax.shard_map(shards, mesh=mesh, in_specs=in_specs, out_specs=out_specs, check_vma=False)
```

profile of v0, /device:TPU:1, one launch (start us, length us, event | category | flops | bytes accessed | tf_op | source)
XLA Modules:
  0.0 901.3 jit_solution(12688166231259519169)
XLA Ops:
  12.8 14.7 %all-reduce.2 = (s32[544]{0:T(1024)S(1)}, s32[544]{0:T(1024)S(1)}) all-reduce(s32[544]{0:T(1024)S(1)} %bitcast_dynamic-update-slice_fusion.1, s32[544]{0:T(1024)S(1)} %bitcast_dynamic-update-slice_fusion), channel_id=2, replica_groups=mesh['fsdp'=32,'tensor'=4] {'fsdp'}, use_global_device_ids=true, to_apply=%add | all-reduce | flops 1088 | bytes 8704
  29.9 6.3 all-gather.8.cloned.1.call-done
  38.5 76.5 %all-gather.10.cloned.1.call-done = bf16[1,544,128,128]{3,2,0,1:T(8,128)(2,1)} async-done(((bf16[1,17,128,128]{3,2,0,1:T(8,128)(2,1)}), bf16[1,544,128,128]{3,2,0,1:T(8,128)(2,1)}) %all-gather.10.cloned.1.call-update) | async-done | bytes 17825808 | tf_op jit(solution)/shard_map/all_gather | solution.py:42
  115.0 76.6 %all-gather.12.cloned.1.call-done = bf16[1,544,128,128]{3,2,0,1:T(8,128)(2,1)} async-done(((bf16[1,17,128,128]{3,2,0,1:T(8,128)(2,1)}), bf16[1,544,128,128]{3,2,0,1:T(8,128)(2,1)}) %all-gather.12.cloned.1.call-update) | async-done | bytes 17825808 | tf_op jit(solution)/shard_map/all_gather | solution.py:44
  193.3 340.1 %while.28 = (s32[]{:T(128)}, f32[128,28,128]{2,0,1:T(8,128)S(1)}, f32[128,28,128]{2,0,1:T(8,128)}, s32[8,68]{1,0:T(8,128)S(1)}, bf16[8,68,128,128]{3,2,1,0:T(8,1...) while((s32[]{:T(128)}, f32[128,28,128]{2,0,1:T(8,128)S(1)}, ...), condition=%wide.region_3.5_spmd, body=%wide.region_0.4_spmd.sunk | while | flops 574887424 | bytes 53490772 | solution.py:66
  201.0 17.0 %scatter_fusion.1 = f32[128,28,128]{2,0,1:T(8,128)} fusion(f32[128,28,128]{2,0,1:T(8,128)} %get-tuple-element.504, s32[68]{0:T(128)S(1)} %get-tuple-element.476, f32[68,128,128]{2,1,0:T(8,128)} %fusion.70), kind=kCustom, calls=%fused_computation.5.clone.1 | custom fusion | flops 1114112 | bytes 13369616 | tf_op jit(solution)/shard_map/while/body/eval_jaxpr/scatter-add | solution.py:20
  220.4 5.2 fusion.69
  225.6 10.6 %scatter_fusion = f32[128,28,128]{2,0,1:T(8,128)S(1)} fusion(f32[128,28,128]{2,0,1:T(8,128)S(1)} %get-tuple-element.503, s32[68]{0:T(128)S(1)} %get-tuple-element.473, f32[68,128,128]{2,1,0:T(8,128)} %fusion.69), kind=kCustom, calls=%fused_computation.4.clone.1 | custom fusion | flops 1114112 | bytes 13369616 | tf_op jit(solution)/shard_map/while/body/eval_jaxpr/scatter-add | solution.py:20
  238.7 5.2 fusion.70
  243.8 16.4 %scatter_fusion.1 = f32[128,28,128]{2,0,1:T(8,128)} fusion(f32[128,28,128]{2,0,1:T(8,128)} %get-tuple-element.504, s32[68]{0:T(128)S(1)} %get-tuple-element.476, f32[68,128,128]{2,1,0:T(8,128)} %fusion.70), kind=kCustom, calls=%fused_computation.5.clone.1 | custom fusion | flops 1114112 | bytes 13369616 | tf_op jit(solution)/shard_map/while/body/eval_jaxpr/scatter-add | solution.py:20
  262.7 5.2 fusion.69
  267.9 10.6 %scatter_fusion = f32[128,28,128]{2,0,1:T(8,128)S(1)} fusion(f32[128,28,128]{2,0,1:T(8,128)S(1)} %get-tuple-element.503, s32[68]{0:T(128)S(1)} %get-tuple-element.473, f32[68,128,128]{2,1,0:T(8,128)} %fusion.69), kind=kCustom, calls=%fused_computation.4.clone.1 | custom fusion | flops 1114112 | bytes 13369616 | tf_op jit(solution)/shard_map/while/body/eval_jaxpr/scatter-add | solution.py:20
  281.0 5.2 fusion.70
  286.2 16.9 %scatter_fusion.1 = f32[128,28,128]{2,0,1:T(8,128)} fusion(f32[128,28,128]{2,0,1:T(8,128)} %get-tuple-element.504, s32[68]{0:T(128)S(1)} %get-tuple-element.476, f32[68,128,128]{2,1,0:T(8,128)} %fusion.70), kind=kCustom, calls=%fused_computation.5.clone.1 | custom fusion | flops 1114112 | bytes 13369616 | tf_op jit(solution)/shard_map/while/body/eval_jaxpr/scatter-add | solution.py:20
  305.5 5.2 fusion.69
  310.7 10.6 %scatter_fusion = f32[128,28,128]{2,0,1:T(8,128)S(1)} fusion(f32[128,28,128]{2,0,1:T(8,128)S(1)} %get-tuple-element.503, s32[68]{0:T(128)S(1)} %get-tuple-element.473, f32[68,128,128]{2,1,0:T(8,128)} %fusion.69), kind=kCustom, calls=%fused_computation.4.clone.1 | custom fusion | flops 1114112 | bytes 13369616 | tf_op jit(solution)/shard_map/while/body/eval_jaxpr/scatter-add | solution.py:20
  323.8 5.2 fusion.70
  329.0 16.4 %scatter_fusion.1 = f32[128,28,128]{2,0,1:T(8,128)} fusion(f32[128,28,128]{2,0,1:T(8,128)} %get-tuple-element.504, s32[68]{0:T(128)S(1)} %get-tuple-element.476, f32[68,128,128]{2,1,0:T(8,128)} %fusion.70), kind=kCustom, calls=%fused_computation.5.clone.1 | custom fusion | flops 1114112 | bytes 13369616 | tf_op jit(solution)/shard_map/while/body/eval_jaxpr/scatter-add | solution.py:20
  353.0 10.6 %scatter_fusion = f32[128,28,128]{2,0,1:T(8,128)S(1)} fusion(f32[128,28,128]{2,0,1:T(8,128)S(1)} %get-tuple-element.503, s32[68]{0:T(128)S(1)} %get-tuple-element.473, f32[68,128,128]{2,1,0:T(8,128)} %fusion.69), kind=kCustom, calls=%fused_computation.4.clone.1 | custom fusion | flops 1114112 | bytes 13369616 | tf_op jit(solution)/shard_map/while/body/eval_jaxpr/scatter-add | solution.py:20
  371.3 16.6 %scatter_fusion.1 = f32[128,28,128]{2,0,1:T(8,128)} fusion(f32[128,28,128]{2,0,1:T(8,128)} %get-tuple-element.504, s32[68]{0:T(128)S(1)} %get-tuple-element.476, f32[68,128,128]{2,1,0:T(8,128)} %fusion.70), kind=kCustom, calls=%fused_computation.5.clone.1 | custom fusion | flops 1114112 | bytes 13369616 | tf_op jit(solution)/shard_map/while/body/eval_jaxpr/scatter-add | solution.py:20
  390.3 5.2 fusion.69
  395.5 10.6 %scatter_fusion = f32[128,28,128]{2,0,1:T(8,128)S(1)} fusion(f32[128,28,128]{2,0,1:T(8,128)S(1)} %get-tuple-element.503, s32[68]{0:T(128)S(1)} %get-tuple-element.473, f32[68,128,128]{2,1,0:T(8,128)} %fusion.69), kind=kCustom, calls=%fused_computation.4.clone.1 | custom fusion | flops 1114112 | bytes 13369616 | tf_op jit(solution)/shard_map/while/body/eval_jaxpr/scatter-add | solution.py:20
  413.8 16.4 %scatter_fusion.1 = f32[128,28,128]{2,0,1:T(8,128)} fusion(f32[128,28,128]{2,0,1:T(8,128)} %get-tuple-element.504, s32[68]{0:T(128)S(1)} %get-tuple-element.476, f32[68,128,128]{2,1,0:T(8,128)} %fusion.70), kind=kCustom, calls=%fused_computation.5.clone.1 | custom fusion | flops 1114112 | bytes 13369616 | tf_op jit(solution)/shard_map/while/body/eval_jaxpr/scatter-add | solution.py:20
  437.8 10.6 %scatter_fusion = f32[128,28,128]{2,0,1:T(8,128)S(1)} fusion(f32[128,28,128]{2,0,1:T(8,128)S(1)} %get-tuple-element.503, s32[68]{0:T(128)S(1)} %get-tuple-element.473, f32[68,128,128]{2,1,0:T(8,128)} %fusion.69), kind=kCustom, calls=%fused_computation.4.clone.1 | custom fusion | flops 1114112 | bytes 13369616 | tf_op jit(solution)/shard_map/while/body/eval_jaxpr/scatter-add | solution.py:20
  456.1 16.4 %scatter_fusion.1 = f32[128,28,128]{2,0,1:T(8,128)} fusion(f32[128,28,128]{2,0,1:T(8,128)} %get-tuple-element.504, s32[68]{0:T(128)S(1)} %get-tuple-element.476, f32[68,128,128]{2,1,0:T(8,128)} %fusion.70), kind=kCustom, calls=%fused_computation.5.clone.1 | custom fusion | flops 1114112 | bytes 13369616 | tf_op jit(solution)/shard_map/while/body/eval_jaxpr/scatter-add | solution.py:20
  475.0 5.2 fusion.69
  480.1 10.6 %scatter_fusion = f32[128,28,128]{2,0,1:T(8,128)S(1)} fusion(f32[128,28,128]{2,0,1:T(8,128)S(1)} %get-tuple-element.503, s32[68]{0:T(128)S(1)} %get-tuple-element.473, f32[68,128,128]{2,1,0:T(8,128)} %fusion.69), kind=kCustom, calls=%fused_computation.4.clone.1 | custom fusion | flops 1114112 | bytes 13369616 | tf_op jit(solution)/shard_map/while/body/eval_jaxpr/scatter-add | solution.py:20
  498.4 16.8 %scatter_fusion.1 = f32[128,28,128]{2,0,1:T(8,128)} fusion(f32[128,28,128]{2,0,1:T(8,128)} %get-tuple-element.504, s32[68]{0:T(128)S(1)} %get-tuple-element.476, f32[68,128,128]{2,1,0:T(8,128)} %fusion.70), kind=kCustom, calls=%fused_computation.5.clone.1 | custom fusion | flops 1114112 | bytes 13369616 | tf_op jit(solution)/shard_map/while/body/eval_jaxpr/scatter-add | solution.py:20
  517.7 5.2 fusion.69
  522.9 10.6 %scatter_fusion = f32[128,28,128]{2,0,1:T(8,128)S(1)} fusion(f32[128,28,128]{2,0,1:T(8,128)S(1)} %get-tuple-element.503, s32[68]{0:T(128)S(1)} %get-tuple-element.473, f32[68,128,128]{2,1,0:T(8,128)} %fusion.69), kind=kCustom, calls=%fused_computation.4.clone.1 | custom fusion | flops 1114112 | bytes 13369616 | tf_op jit(solution)/shard_map/while/body/eval_jaxpr/scatter-add | solution.py:20
  545.3 315.6 %while.29 = (s32[]{:T(128)}, f32[128,32,128]{2,0,1:T(8,128)S(1)}, s32[8,68]{1,0:T(8,128)S(1)}, bf16[8,68,128,128]{3,2,1,0:T(8,128)(2,1)}, bf16[128,28,128]{2,0,1...) while((s32[]{:T(128)}, f32[128,32,128]{2,0,1:T(8,128)S(1)}, ...), condition=%wide.region_7.10_spmd, body=%wide.region_4.9_spmd.sunk | while | flops 574887424 | bytes 53490772 | solution.py:86
  548.0 6.1 fusion.76
  554.1 10.6 %scatter_fusion.2 = f32[128,32,128]{2,0,1:T(8,128)S(1)} fusion(f32[128,32,128]{2,0,1:T(8,128)S(1)} %get-tuple-element.530, s32[68]{0:T(128)S(1)} %get-tuple-element.487, f32[68,128,128]{2,1,0:T(8,128)} %fusion.76), kind=kCustom, calls=%fused_computation.6.clone.1 | custom fusion | flops 1114112 | bytes 13369616 | tf_op jit(solution)/shard_map/while/body/eval_jaxpr/scatter-add | solution.py:27
  568.3 6.1 fusion.77
  574.4 10.5 %scatter_fusion.3 = f32[128,32,128]{2,0,1:T(8,128)S(1)} fusion(f32[128,32,128]{2,0,1:T(8,128)S(1)} %scatter_fusion.2, s32[68]{0:T(128)S(1)} %get-tuple-element.490, f32[68,128,128]{2,1,0:T(8,128)} %fusion.77), kind=kCustom, calls=%fused_computation.7.clone.1 | custom fusion | flops 1114112 | bytes 13369616 | tf_op jit(solution)/shard_map/while/body/eval_jaxpr/scatter-add | solution.py:27
  587.4 6.1 fusion.76
  593.5 10.6 %scatter_fusion.2 = f32[128,32,128]{2,0,1:T(8,128)S(1)} fusion(f32[128,32,128]{2,0,1:T(8,128)S(1)} %get-tuple-element.530, s32[68]{0:T(128)S(1)} %get-tuple-element.487, f32[68,128,128]{2,1,0:T(8,128)} %fusion.76), kind=kCustom, calls=%fused_computation.6.clone.1 | custom fusion | flops 1114112 | bytes 13369616 | tf_op jit(solution)/shard_map/while/body/eval_jaxpr/scatter-add | solution.py:27
  607.7 6.1 fusion.77
  613.8 10.5 %scatter_fusion.3 = f32[128,32,128]{2,0,1:T(8,128)S(1)} fusion(f32[128,32,128]{2,0,1:T(8,128)S(1)} %scatter_fusion.2, s32[68]{0:T(128)S(1)} %get-tuple-element.490, f32[68,128,128]{2,1,0:T(8,128)} %fusion.77), kind=kCustom, calls=%fused_computation.7.clone.1 | custom fusion | flops 1114112 | bytes 13369616 | tf_op jit(solution)/shard_map/while/body/eval_jaxpr/scatter-add | solution.py:27
  626.8 6.1 fusion.76
  632.9 10.6 %scatter_fusion.2 = f32[128,32,128]{2,0,1:T(8,128)S(1)} fusion(f32[128,32,128]{2,0,1:T(8,128)S(1)} %get-tuple-element.530, s32[68]{0:T(128)S(1)} %get-tuple-element.487, f32[68,128,128]{2,1,0:T(8,128)} %fusion.76), kind=kCustom, calls=%fused_computation.6.clone.1 | custom fusion | flops 1114112 | bytes 13369616 | tf_op jit(solution)/shard_map/while/body/eval_jaxpr/scatter-add | solution.py:27
  647.1 6.1 fusion.77
  653.2 10.6 %scatter_fusion.3 = f32[128,32,128]{2,0,1:T(8,128)S(1)} fusion(f32[128,32,128]{2,0,1:T(8,128)S(1)} %scatter_fusion.2, s32[68]{0:T(128)S(1)} %get-tuple-element.490, f32[68,128,128]{2,1,0:T(8,128)} %fusion.77), kind=kCustom, calls=%fused_computation.7.clone.1 | custom fusion | flops 1114112 | bytes 13369616 | tf_op jit(solution)/shard_map/while/body/eval_jaxpr/scatter-add | solution.py:27
  666.3 6.1 fusion.76
  672.4 10.6 %scatter_fusion.2 = f32[128,32,128]{2,0,1:T(8,128)S(1)} fusion(f32[128,32,128]{2,0,1:T(8,128)S(1)} %get-tuple-element.530, s32[68]{0:T(128)S(1)} %get-tuple-element.487, f32[68,128,128]{2,1,0:T(8,128)} %fusion.76), kind=kCustom, calls=%fused_computation.6.clone.1 | custom fusion | flops 1114112 | bytes 13369616 | tf_op jit(solution)/shard_map/while/body/eval_jaxpr/scatter-add | solution.py:27
  686.6 6.1 fusion.77
  692.7 10.6 %scatter_fusion.3 = f32[128,32,128]{2,0,1:T(8,128)S(1)} fusion(f32[128,32,128]{2,0,1:T(8,128)S(1)} %scatter_fusion.2, s32[68]{0:T(128)S(1)} %get-tuple-element.490, f32[68,128,128]{2,1,0:T(8,128)} %fusion.77), kind=kCustom, calls=%fused_computation.7.clone.1 | custom fusion | flops 1114112 | bytes 13369616 | tf_op jit(solution)/shard_map/while/body/eval_jaxpr/scatter-add | solution.py:27
  705.7 6.1 fusion.76
  711.8 10.6 %scatter_fusion.2 = f32[128,32,128]{2,0,1:T(8,128)S(1)} fusion(f32[128,32,128]{2,0,1:T(8,128)S(1)} %get-tuple-element.530, s32[68]{0:T(128)S(1)} %get-tuple-element.487, f32[68,128,128]{2,1,0:T(8,128)} %fusion.76), kind=kCustom, calls=%fused_computation.6.clone.1 | custom fusion | flops 1114112 | bytes 13369616 | tf_op jit(solution)/shard_map/while/body/eval_jaxpr/scatter-add | solution.py:27
  726.0 6.1 fusion.77
  732.1 10.6 %scatter_fusion.3 = f32[128,32,128]{2,0,1:T(8,128)S(1)} fusion(f32[128,32,128]{2,0,1:T(8,128)S(1)} %scatter_fusion.2, s32[68]{0:T(128)S(1)} %get-tuple-element.490, f32[68,128,128]{2,1,0:T(8,128)} %fusion.77), kind=kCustom, calls=%fused_computation.7.clone.1 | custom fusion | flops 1114112 | bytes 13369616 | tf_op jit(solution)/shard_map/while/body/eval_jaxpr/scatter-add | solution.py:27
  745.1 6.1 fusion.76
  751.2 10.6 %scatter_fusion.2 = f32[128,32,128]{2,0,1:T(8,128)S(1)} fusion(f32[128,32,128]{2,0,1:T(8,128)S(1)} %get-tuple-element.530, s32[68]{0:T(128)S(1)} %get-tuple-element.487, f32[68,128,128]{2,1,0:T(8,128)} %fusion.76), kind=kCustom, calls=%fused_computation.6.clone.1 | custom fusion | flops 1114112 | bytes 13369616 | tf_op jit(solution)/shard_map/while/body/eval_jaxpr/scatter-add | solution.py:27
  765.4 6.1 fusion.77
  771.5 10.6 %scatter_fusion.3 = f32[128,32,128]{2,0,1:T(8,128)S(1)} fusion(f32[128,32,128]{2,0,1:T(8,128)S(1)} %scatter_fusion.2, s32[68]{0:T(128)S(1)} %get-tuple-element.490, f32[68,128,128]{2,1,0:T(8,128)} %fusion.77), kind=kCustom, calls=%fused_computation.7.clone.1 | custom fusion | flops 1114112 | bytes 13369616 | tf_op jit(solution)/shard_map/while/body/eval_jaxpr/scatter-add | solution.py:27
  784.6 6.1 fusion.76
  790.7 10.6 %scatter_fusion.2 = f32[128,32,128]{2,0,1:T(8,128)S(1)} fusion(f32[128,32,128]{2,0,1:T(8,128)S(1)} %get-tuple-element.530, s32[68]{0:T(128)S(1)} %get-tuple-element.487, f32[68,128,128]{2,1,0:T(8,128)} %fusion.76), kind=kCustom, calls=%fused_computation.6.clone.1 | custom fusion | flops 1114112 | bytes 13369616 | tf_op jit(solution)/shard_map/while/body/eval_jaxpr/scatter-add | solution.py:27
  804.9 6.1 fusion.77
  811.0 10.6 %scatter_fusion.3 = f32[128,32,128]{2,0,1:T(8,128)S(1)} fusion(f32[128,32,128]{2,0,1:T(8,128)S(1)} %scatter_fusion.2, s32[68]{0:T(128)S(1)} %get-tuple-element.490, f32[68,128,128]{2,1,0:T(8,128)} %fusion.77), kind=kCustom, calls=%fused_computation.7.clone.1 | custom fusion | flops 1114112 | bytes 13369616 | tf_op jit(solution)/shard_map/while/body/eval_jaxpr/scatter-add | solution.py:27
  824.0 6.1 fusion.76
  830.1 10.6 %scatter_fusion.2 = f32[128,32,128]{2,0,1:T(8,128)S(1)} fusion(f32[128,32,128]{2,0,1:T(8,128)S(1)} %get-tuple-element.530, s32[68]{0:T(128)S(1)} %get-tuple-element.487, f32[68,128,128]{2,1,0:T(8,128)} %fusion.76), kind=kCustom, calls=%fused_computation.6.clone.1 | custom fusion | flops 1114112 | bytes 13369616 | tf_op jit(solution)/shard_map/while/body/eval_jaxpr/scatter-add | solution.py:27
  844.3 6.1 fusion.77
  850.4 10.5 %scatter_fusion.3 = f32[128,32,128]{2,0,1:T(8,128)S(1)} fusion(f32[128,32,128]{2,0,1:T(8,128)S(1)} %scatter_fusion.2, s32[68]{0:T(128)S(1)} %get-tuple-element.490, f32[68,128,128]{2,1,0:T(8,128)} %fusion.77), kind=kCustom, calls=%fused_computation.7.clone.1 | custom fusion | flops 1114112 | bytes 13369616 | tf_op jit(solution)/shard_map/while/body/eval_jaxpr/scatter-add | solution.py:27
  863.8 29.2 %reduce-scatter.2.cloned.1.call-done = f32[32,4096]{1,0:T(8,128)} async-done(((f32[128,4096]{1,0:T(8,128)}), f32[32,4096]{1,0:T(8,128)}) %reduce-scatter.2.cloned.1.call-update) | async-done | bytes 524304 | tf_op jit(solution)/shard_map/reduce_scatter | solution.py:88
  (140 shorter events, 152.4 us)
Async XLA Ops:
  7.2 29.0 %all-gather.8.cloned.1.call-start = ((), (), s32[]{:S(2)}) async-start(), calls=%async_computation.1 | async-start | bytes 1310720 | tf_op jit(solution)/shard_map/all_gather | solution.py:32
  7.9 107.1 %all-gather.10.cloned.1.call-start = ((), (), s32[]{:S(2)}) async-start(), calls=%async_computation.3 | async-start | bytes 18382848 | tf_op jit(solution)/shard_map/all_gather | solution.py:42
  8.6 183.0 %all-gather.12.cloned.1.call-start = ((), (), s32[]{:S(2)}) async-start(), calls=%async_computation.4 | async-start | bytes 18382848 | tf_op jit(solution)/shard_map/all_gather | solution.py:44
  9.4 883.6 %reduce-scatter.2.cloned.1.call-start = ((), (), s32[]{:S(2)}) async-start(), calls=%async_computation.2 | async-start | bytes 2621440 | tf_op jit(solution)/shard_map/reduce_scatter | solution.py:88
  535.2 2.9 copy-start
  535.2 2.9 copy-start.1
  542.2 1.7 copy-start.3
  860.9 1.6 copy-start.2
Sparse Core Ops, SparseCore 0:
  9.7 26.4 all-gather.7
  38.4 76.5 all-gather.9
  117.3 74.3 all-gather.11
  862.7 30.2 reduce-scatter.1
where the time goes:
time: 908 us; the launch traced here: 901 us
  other arithmetic  393 us (43%)
  waiting for transfers between devices  191 us (21%)
  matrix products  180 us (20%)
  local copies, waits for them, and re-layouts  107 us (12%)
  blocking collectives  14.7 us (2%)
  between operations  14.5 us (2%)
    scatter-add x16, other arithmetic, forward_group(): return total.at[:, col_target].add(product, mode='drop')  218 us
    scatter-add x16, other arithmetic, backward_group(): return total.at[:, row_target].add(product, mode='drop')  169 us
    dot_general x16, matrix products, backward_group(): jnp.einsum('tsn,skn->tsk', chosen, blocks, preferred_element_type=jnp.flo...  97.2 us
    dot_general x16, matrix products, forward_group(): jnp.einsum('tsk,skn->tsn', picked, blocks, preferred_element_type=jnp.flo...  82.6 us
    all_gather x1, waiting for transfers between devices, shards(): lax.all_gather(own_up, 'fsdp', axis=0, tiled=True)  76.6 us
    all_gather x1, waiting for transfers between devices, shards(): lax.all_gather(own_gate, 'fsdp', axis=0, tiled=True)  76.5 us
    gather x16, local copies, waits for them, and re-layouts, backward_group(): chosen = jnp.take(grad_split, col_of, axis=1)  48.5 us
    gather x16, local copies, waits for them, and re-layouts, forward_group(): picked = jnp.take(rows_split, row_of, axis=1)  39 us
  transfers between devices with their start and end apart: 4, of which 4 were waited for; matrix products, arithmetic and copies ran while one was open for 1% of the time, Pallas kernels for 0%

commit v1 on v0

--- a/solution.py
+++ b/solution.py
@@ -2,6 +2,13 @@
 import jax.numpy as jnp
 from jax import lax
 from jax.sharding import PartitionSpec as P
+
+
+def swapped_in(x, axis, dim):
+    n_dev = lax.axis_size(axis)
+    tiles = jnp.stack([x for _ in range(n_dev)])
+    tiles = lax.all_to_all(tiles, axis, split_axis=0, concat_axis=0)
+    return jnp.concatenate(tiles, axis=dim)
 
 
 def positions(block_index, row_blocks, col_blocks):
@@ -41,7 +48,7 @@
     all_gate, all_gate_index, all_up, all_up_index = (
         lax.all_gather(own_gate, "fsdp", axis=0, tiled=True),
         lax.all_gather(own_gate_index, "fsdp", axis=0, tiled=True),
-        lax.all_gather(own_up, "fsdp", axis=0, tiled=True),
+        swapped_in(own_up, "fsdp", 0),
         lax.all_gather(own_up_index, "fsdp", axis=0, tiled=True),
     )
     per_shard = own_gate.shape[0]

time: 908 us -> 1050 us (1.16)
  blocking collectives: 14.7 us -> 263 us
  waiting for transfers between devices: 191 us -> 77.5 us
    unnamed x1, blocking collectives: 14.7 us -> 263 us
    all_gather x1 -> x0, waiting for transfers between devices: 76.6 us -> none  [shards(): lax.all_gather(own_up, 'fsdp', axis=0, tiled=True)]
    all_gather x1, waiting for transfers between devices: 76.5 us -> 0.01 us  [shards(): lax.all_gather(own_gate, 'fsdp', axis=0, tiled=True)]
    reduce_scatter x1, waiting for transfers between devices: 29.2 us -> 68.6 us  [shards(): lax.psum_scatter(partial_grad, 'tensor', scatter_dimension=0, tiled=True)]
  transfers between devices with their start and end apart: 4 -> 4, of which waited for: 4 -> 2; matrix products, arithmetic and copies ran while one was open for 1% -> 1% of each run, Pallas kernels for 0% -> 0%
where the time goes in v1:
time: 1050 us
  other arithmetic  390 us (37%)
  blocking collectives  263 us (25%)
  matrix products  179 us (17%)
  local copies, waits for them, and re-layouts  112 us (11%)
  waiting for transfers between devices  77.5 us (7%)
  between operations  14.5 us (1%)
    unnamed x1, blocking collectives  263 us
    scatter-add x16, other arithmetic, forward_group(): return total.at[:, col_target].add(product, mode='drop')  214 us
    scatter-add x16, other arithmetic, backward_group(): return total.at[:, row_target].add(product, mode='drop')  169 us
    dot_general x16, matrix products, backward_group(): jnp.einsum('tsn,skn->tsk', chosen, blocks, preferred_element_type=jnp.flo...  97 us
    dot_general x16, matrix products, forward_group(): jnp.einsum('tsk,skn->tsn', picked, blocks, preferred_element_type=jnp.flo...  82.4 us
    reduce_scatter x1, waiting for transfers between devices, shards(): lax.psum_scatter(partial_grad, 'tensor', scatter_dimension=0, tiled=True)  68.6 us
    gather x16, local copies, waits for them, and re-layouts, backward_group(): chosen = jnp.take(grad_split, col_of, axis=1)  48.4 us
    gather x16, local copies, waits for them, and re-layouts, forward_group(): picked = jnp.take(rows_split, row_of, axis=1)  39 us
  transfers between devices with their start and end apart: 4, of which 2 were waited for; matrix products, arithmetic and copies ran while one was open for 1% of the time, Pallas kernels for 0%

profile of v1, /device:TPU:1, one launch (start us, length us, event | category | flops | bytes accessed | tf_op | source)
XLA Modules:
  0.0 1046.2 jit_solution(4213315728137728349)
XLA Ops:
  8.6 7.3 stack.3
  16.0 8.8 all-to-all-start
  26.3 263.2 %all-reduce.2 = (s32[544]{0:T(1024)S(1)}, s32[544]{0:T(1024)S(1)}) all-reduce(s32[544]{0:T(1024)S(1)} %bitcast_dynamic-update-slice_fusion.1, s32[544]{0:T(1024)S(1)} %bitcast_dynamic-update-slice_fusion), channel_id=2, replica_groups=mesh['fsdp'=32,'tensor'=4] {'fsdp'}, use_global_device_ids=true, to_apply=%add | all-reduce | flops 1088 | bytes 8704
  293.2 7.5 all-to-all-done
  302.5 336.7 %while.28 = (s32[]{:T(128)}, f32[128,28,128]{2,0,1:T(8,128)S(1)}, f32[128,28,128]{2,0,1:T(8,128)}, s32[8,68]{1,0:T(8,128)S(1)}, bf16[8,68,128,128]{3,2,1,0:T(8,1...) while((s32[]{:T(128)}, f32[128,28,128]{2,0,1:T(8,128)S(1)}, ...), condition=%wide.region_3.5_spmd, body=%wide.region_0.4_spmd.sunk | while | flops 574887424 | bytes 53490772 | solution.py:73
  305.0 5.2 fusion.70
  310.1 16.5 %scatter_fusion.1 = f32[128,28,128]{2,0,1:T(8,128)} fusion(f32[128,28,128]{2,0,1:T(8,128)} %get-tuple-element.504, s32[68]{0:T(128)S(1)} %get-tuple-element.476, f32[68,128,128]{2,1,0:T(8,128)} %fusion.70), kind=kCustom, calls=%fused_computation.5.clone.1 | custom fusion | flops 1114112 | bytes 13369616 | tf_op jit(solution)/shard_map/while/body/eval_jaxpr/scatter-add | solution.py:27
  329.1 5.2 fusion.69
  334.3 10.6 %scatter_fusion = f32[128,28,128]{2,0,1:T(8,128)S(1)} fusion(f32[128,28,128]{2,0,1:T(8,128)S(1)} %get-tuple-element.503, s32[68]{0:T(128)S(1)} %get-tuple-element.473, f32[68,128,128]{2,1,0:T(8,128)} %fusion.69), kind=kCustom, calls=%fused_computation.4.clone.1 | custom fusion | flops 1114112 | bytes 13369616 | tf_op jit(solution)/shard_map/while/body/eval_jaxpr/scatter-add | solution.py:27
  347.4 5.2 fusion.70
  352.5 16.1 %scatter_fusion.1 = f32[128,28,128]{2,0,1:T(8,128)} fusion(f32[128,28,128]{2,0,1:T(8,128)} %get-tuple-element.504, s32[68]{0:T(128)S(1)} %get-tuple-element.476, f32[68,128,128]{2,1,0:T(8,128)} %fusion.70), kind=kCustom, calls=%fused_computation.5.clone.1 | custom fusion | flops 1114112 | bytes 13369616 | tf_op jit(solution)/shard_map/while/body/eval_jaxpr/scatter-add | solution.py:27
  371.1 5.2 fusion.69
  376.2 10.6 %scatter_fusion = f32[128,28,128]{2,0,1:T(8,128)S(1)} fusion(f32[128,28,128]{2,0,1:T(8,128)S(1)} %get-tuple-element.503, s32[68]{0:T(128)S(1)} %get-tuple-element.473, f32[68,128,128]{2,1,0:T(8,128)} %fusion.69), kind=kCustom, calls=%fused_computation.4.clone.1 | custom fusion | flops 1114112 | bytes 13369616 | tf_op jit(solution)/shard_map/while/body/eval_jaxpr/scatter-add | solution.py:27
  389.3 5.2 fusion.70
  394.5 16.5 %scatter_fusion.1 = f32[128,28,128]{2,0,1:T(8,128)} fusion(f32[128,28,128]{2,0,1:T(8,128)} %get-tuple-element.504, s32[68]{0:T(128)S(1)} %get-tuple-element.476, f32[68,128,128]{2,1,0:T(8,128)} %fusion.70), kind=kCustom, calls=%fused_computation.5.clone.1 | custom fusion | flops 1114112 | bytes 13369616 | tf_op jit(solution)/shard_map/while/body/eval_jaxpr/scatter-add | solution.py:27
  413.4 5.2 fusion.69
  418.6 10.6 %scatter_fusion = f32[128,28,128]{2,0,1:T(8,128)S(1)} fusion(f32[128,28,128]{2,0,1:T(8,128)S(1)} %get-tuple-element.503, s32[68]{0:T(128)S(1)} %get-tuple-element.473, f32[68,128,128]{2,1,0:T(8,128)} %fusion.69), kind=kCustom, calls=%fused_computation.4.clone.1 | custom fusion | flops 1114112 | bytes 13369616 | tf_op jit(solution)/shard_map/while/body/eval_jaxpr/scatter-add | solution.py:27
  431.6 5.2 fusion.70
  436.8 16.1 %scatter_fusion.1 = f32[128,28,128]{2,0,1:T(8,128)} fusion(f32[128,28,128]{2,0,1:T(8,128)} %get-tuple-element.504, s32[68]{0:T(128)S(1)} %get-tuple-element.476, f32[68,128,128]{2,1,0:T(8,128)} %fusion.70), kind=kCustom, calls=%fused_computation.5.clone.1 | custom fusion | flops 1114112 | bytes 13369616 | tf_op jit(solution)/shard_map/while/body/eval_jaxpr/scatter-add | solution.py:27
  460.5 10.6 %scatter_fusion = f32[128,28,128]{2,0,1:T(8,128)S(1)} fusion(f32[128,28,128]{2,0,1:T(8,128)S(1)} %get-tuple-element.503, s32[68]{0:T(128)S(1)} %get-tuple-element.473, f32[68,128,128]{2,1,0:T(8,128)} %fusion.69), kind=kCustom, calls=%fused_computation.4.clone.1 | custom fusion | flops 1114112 | bytes 13369616 | tf_op jit(solution)/shard_map/while/body/eval_jaxpr/scatter-add | solution.py:27
  478.8 16.1 %scatter_fusion.1 = f32[128,28,128]{2,0,1:T(8,128)} fusion(f32[128,28,128]{2,0,1:T(8,128)} %get-tuple-element.504, s32[68]{0:T(128)S(1)} %get-tuple-element.476, f32[68,128,128]{2,1,0:T(8,128)} %fusion.70), kind=kCustom, calls=%fused_computation.5.clone.1 | custom fusion | flops 1114112 | bytes 13369616 | tf_op jit(solution)/shard_map/while/body/eval_jaxpr/scatter-add | solution.py:27
  502.4 10.6 %scatter_fusion = f32[128,28,128]{2,0,1:T(8,128)S(1)} fusion(f32[128,28,128]{2,0,1:T(8,128)S(1)} %get-tuple-element.503, s32[68]{0:T(128)S(1)} %get-tuple-element.473, f32[68,128,128]{2,1,0:T(8,128)} %fusion.69), kind=kCustom, calls=%fused_computation.4.clone.1 | custom fusion | flops 1114112 | bytes 13369616 | tf_op jit(solution)/shard_map/while/body/eval_jaxpr/scatter-add | solution.py:27
  515.5 5.2 fusion.70
  520.7 16.0 %scatter_fusion.1 = f32[128,28,128]{2,0,1:T(8,128)} fusion(f32[128,28,128]{2,0,1:T(8,128)} %get-tuple-element.504, s32[68]{0:T(128)S(1)} %get-tuple-element.476, f32[68,128,128]{2,1,0:T(8,128)} %fusion.70), kind=kCustom, calls=%fused_computation.5.clone.1 | custom fusion | flops 1114112 | bytes 13369616 | tf_op jit(solution)/shard_map/while/body/eval_jaxpr/scatter-add | solution.py:27
  544.3 10.6 %scatter_fusion = f32[128,28,128]{2,0,1:T(8,128)S(1)} fusion(f32[128,28,128]{2,0,1:T(8,128)S(1)} %get-tuple-element.503, s32[68]{0:T(128)S(1)} %get-tuple-element.473, f32[68,128,128]{2,1,0:T(8,128)} %fusion.69), kind=kCustom, calls=%fused_computation.4.clone.1 | custom fusion | flops 1114112 | bytes 13369616 | tf_op jit(solution)/shard_map/while/body/eval_jaxpr/scatter-add | solution.py:27
  557.4 5.2 fusion.70
  562.6 16.1 %scatter_fusion.1 = f32[128,28,128]{2,0,1:T(8,128)} fusion(f32[128,28,128]{2,0,1:T(8,128)} %get-tuple-element.504, s32[68]{0:T(128)S(1)} %get-tuple-element.476, f32[68,128,128]{2,1,0:T(8,128)} %fusion.70), kind=kCustom, calls=%fused_computation.5.clone.1 | custom fusion | flops 1114112 | bytes 13369616 | tf_op jit(solution)/shard_map/while/body/eval_jaxpr/scatter-add | solution.py:27
  586.3 10.6 %scatter_fusion = f32[128,28,128]{2,0,1:T(8,128)S(1)} fusion(f32[128,28,128]{2,0,1:T(8,128)S(1)} %get-tuple-element.503, s32[68]{0:T(128)S(1)} %get-tuple-element.473, f32[68,128,128]{2,1,0:T(8,128)} %fusion.69), kind=kCustom, calls=%fused_computation.4.clone.1 | custom fusion | flops 1114112 | bytes 13369616 | tf_op jit(solution)/shard_map/while/body/eval_jaxpr/scatter-add | solution.py:27
  604.6 16.4 %scatter_fusion.1 = f32[128,28,128]{2,0,1:T(8,128)} fusion(f32[128,28,128]{2,0,1:T(8,128)} %get-tuple-element.504, s32[68]{0:T(128)S(1)} %get-tuple-element.476, f32[68,128,128]{2,1,0:T(8,128)} %fusion.70), kind=kCustom, calls=%fused_computation.5.clone.1 | custom fusion | flops 1114112 | bytes 13369616 | tf_op jit(solution)/shard_map/while/body/eval_jaxpr/scatter-add | solution.py:27
  628.6 10.6 %scatter_fusion = f32[128,28,128]{2,0,1:T(8,128)S(1)} fusion(f32[128,28,128]{2,0,1:T(8,128)S(1)} %get-tuple-element.503, s32[68]{0:T(128)S(1)} %get-tuple-element.473, f32[68,128,128]{2,1,0:T(8,128)} %fusion.69), kind=kCustom, calls=%fused_computation.4.clone.1 | custom fusion | flops 1114112 | bytes 13369616 | tf_op jit(solution)/shard_map/while/body/eval_jaxpr/scatter-add | solution.py:27
  651.0 315.3 %while.29 = (s32[]{:T(128)}, f32[128,32,128]{2,0,1:T(8,128)S(1)}, s32[8,68]{1,0:T(8,128)S(1)}, bf16[8,68,128,128]{3,2,1,0:T(8,128)(2,1)}, bf16[128,28,128]{2,0,1...) while((s32[]{:T(128)}, f32[128,32,128]{2,0,1:T(8,128)S(1)}, ...), condition=%wide.region_7.10_spmd, body=%wide.region_4.9_spmd.sunk | while | flops 574887424 | bytes 53490772 | solution.py:93
  653.7 6.1 fusion.76
  659.8 10.6 %scatter_fusion.2 = f32[128,32,128]{2,0,1:T(8,128)S(1)} fusion(f32[128,32,128]{2,0,1:T(8,128)S(1)} %get-tuple-element.530, s32[68]{0:T(128)S(1)} %get-tuple-element.487, f32[68,128,128]{2,1,0:T(8,128)} %fusion.76), kind=kCustom, calls=%fused_computation.6.clone.1 | custom fusion | flops 1114112 | bytes 13369616 | tf_op jit(solution)/shard_map/while/body/eval_jaxpr/scatter-add | solution.py:34
  674.0 6.1 fusion.77
  680.0 10.5 %scatter_fusion.3 = f32[128,32,128]{2,0,1:T(8,128)S(1)} fusion(f32[128,32,128]{2,0,1:T(8,128)S(1)} %scatter_fusion.2, s32[68]{0:T(128)S(1)} %get-tuple-element.490, f32[68,128,128]{2,1,0:T(8,128)} %fusion.77), kind=kCustom, calls=%fused_computation.7.clone.1 | custom fusion | flops 1114112 | bytes 13369616 | tf_op jit(solution)/shard_map/while/body/eval_jaxpr/scatter-add | solution.py:34
  693.1 6.1 fusion.76
  699.2 10.6 %scatter_fusion.2 = f32[128,32,128]{2,0,1:T(8,128)S(1)} fusion(f32[128,32,128]{2,0,1:T(8,128)S(1)} %get-tuple-element.530, s32[68]{0:T(128)S(1)} %get-tuple-element.487, f32[68,128,128]{2,1,0:T(8,128)} %fusion.76), kind=kCustom, calls=%fused_computation.6.clone.1 | custom fusion | flops 1114112 | bytes 13369616 | tf_op jit(solution)/shard_map/while/body/eval_jaxpr/scatter-add | solution.py:34
  713.4 6.1 fusion.77
  719.4 10.5 %scatter_fusion.3 = f32[128,32,128]{2,0,1:T(8,128)S(1)} fusion(f32[128,32,128]{2,0,1:T(8,128)S(1)} %scatter_fusion.2, s32[68]{0:T(128)S(1)} %get-tuple-element.490, f32[68,128,128]{2,1,0:T(8,128)} %fusion.77), kind=kCustom, calls=%fused_computation.7.clone.1 | custom fusion | flops 1114112 | bytes 13369616 | tf_op jit(solution)/shard_map/while/body/eval_jaxpr/scatter-add | solution.py:34
  732.5 6.1 fusion.76
  738.6 10.6 %scatter_fusion.2 = f32[128,32,128]{2,0,1:T(8,128)S(1)} fusion(f32[128,32,128]{2,0,1:T(8,128)S(1)} %get-tuple-element.530, s32[68]{0:T(128)S(1)} %get-tuple-element.487, f32[68,128,128]{2,1,0:T(8,128)} %fusion.76), kind=kCustom, calls=%fused_computation.6.clone.1 | custom fusion | flops 1114112 | bytes 13369616 | tf_op jit(solution)/shard_map/while/body/eval_jaxpr/scatter-add | solution.py:34
  752.8 6.1 fusion.77
  758.8 10.6 %scatter_fusion.3 = f32[128,32,128]{2,0,1:T(8,128)S(1)} fusion(f32[128,32,128]{2,0,1:T(8,128)S(1)} %scatter_fusion.2, s32[68]{0:T(128)S(1)} %get-tuple-element.490, f32[68,128,128]{2,1,0:T(8,128)} %fusion.77), kind=kCustom, calls=%fused_computation.7.clone.1 | custom fusion | flops 1114112 | bytes 13369616 | tf_op jit(solution)/shard_map/while/body/eval_jaxpr/scatter-add | solution.py:34
  771.9 6.1 fusion.76
  778.0 10.6 %scatter_fusion.2 = f32[128,32,128]{2,0,1:T(8,128)S(1)} fusion(f32[128,32,128]{2,0,1:T(8,128)S(1)} %get-tuple-element.530, s32[68]{0:T(128)S(1)} %get-tuple-element.487, f32[68,128,128]{2,1,0:T(8,128)} %fusion.76), kind=kCustom, calls=%fused_computation.6.clone.1 | custom fusion | flops 1114112 | bytes 13369616 | tf_op jit(solution)/shard_map/while/body/eval_jaxpr/scatter-add | solution.py:34
  792.2 6.1 fusion.77
  798.2 10.6 %scatter_fusion.3 = f32[128,32,128]{2,0,1:T(8,128)S(1)} fusion(f32[128,32,128]{2,0,1:T(8,128)S(1)} %scatter_fusion.2, s32[68]{0:T(128)S(1)} %get-tuple-element.490, f32[68,128,128]{2,1,0:T(8,128)} %fusion.77), kind=kCustom, calls=%fused_computation.7.clone.1 | custom fusion | flops 1114112 | bytes 13369616 | tf_op jit(solution)/shard_map/while/body/eval_jaxpr/scatter-add | solution.py:34
  811.3 6.1 fusion.76
  817.4 10.6 %scatter_fusion.2 = f32[128,32,128]{2,0,1:T(8,128)S(1)} fusion(f32[128,32,128]{2,0,1:T(8,128)S(1)} %get-tuple-element.530, s32[68]{0:T(128)S(1)} %get-tuple-element.487, f32[68,128,128]{2,1,0:T(8,128)} %fusion.76), kind=kCustom, calls=%fused_computation.6.clone.1 | custom fusion | flops 1114112 | bytes 13369616 | tf_op jit(solution)/shard_map/while/body/eval_jaxpr/scatter-add | solution.py:34
  831.6 6.1 fusion.77
  837.6 10.6 %scatter_fusion.3 = f32[128,32,128]{2,0,1:T(8,128)S(1)} fusion(f32[128,32,128]{2,0,1:T(8,128)S(1)} %scatter_fusion.2, s32[68]{0:T(128)S(1)} %get-tuple-element.490, f32[68,128,128]{2,1,0:T(8,128)} %fusion.77), kind=kCustom, calls=%fused_computation.7.clone.1 | custom fusion | flops 1114112 | bytes 13369616 | tf_op jit(solution)/shard_map/while/body/eval_jaxpr/scatter-add | solution.py:34
  850.7 6.1 fusion.76
  856.8 10.6 %scatter_fusion.2 = f32[128,32,128]{2,0,1:T(8,128)S(1)} fusion(f32[128,32,128]{2,0,1:T(8,128)S(1)} %get-tuple-element.530, s32[68]{0:T(128)S(1)} %get-tuple-element.487, f32[68,128,128]{2,1,0:T(8,128)} %fusion.76), kind=kCustom, calls=%fused_computation.6.clone.1 | custom fusion | flops 1114112 | bytes 13369616 | tf_op jit(solution)/shard_map/while/body/eval_jaxpr/scatter-add | solution.py:34
  871.0 6.1 fusion.77
  877.0 10.6 %scatter_fusion.3 = f32[128,32,128]{2,0,1:T(8,128)S(1)} fusion(f32[128,32,128]{2,0,1:T(8,128)S(1)} %scatter_fusion.2, s32[68]{0:T(128)S(1)} %get-tuple-element.490, f32[68,128,128]{2,1,0:T(8,128)} %fusion.77), kind=kCustom, calls=%fused_computation.7.clone.1 | custom fusion | flops 1114112 | bytes 13369616 | tf_op jit(solution)/shard_map/while/body/eval_jaxpr/scatter-add | solution.py:34
  890.1 6.1 fusion.76
  896.2 10.6 %scatter_fusion.2 = f32[128,32,128]{2,0,1:T(8,128)S(1)} fusion(f32[128,32,128]{2,0,1:T(8,128)S(1)} %get-tuple-element.530, s32[68]{0:T(128)S(1)} %get-tuple-element.487, f32[68,128,128]{2,1,0:T(8,128)} %fusion.76), kind=kCustom, calls=%fused_computation.6.clone.1 | custom fusion | flops 1114112 | bytes 13369616 | tf_op jit(solution)/shard_map/while/body/eval_jaxpr/scatter-add | solution.py:34
  910.4 6.1 fusion.77
  916.4 10.6 %scatter_fusion.3 = f32[128,32,128]{2,0,1:T(8,128)S(1)} fusion(f32[128,32,128]{2,0,1:T(8,128)S(1)} %scatter_fusion.2, s32[68]{0:T(128)S(1)} %get-tuple-element.490, f32[68,128,128]{2,1,0:T(8,128)} %fusion.77), kind=kCustom, calls=%fused_computation.7.clone.1 | custom fusion | flops 1114112 | bytes 13369616 | tf_op jit(solution)/shard_map/while/body/eval_jaxpr/scatter-add | solution.py:34
  929.5 6.1 fusion.76
  935.6 10.6 %scatter_fusion.2 = f32[128,32,128]{2,0,1:T(8,128)S(1)} fusion(f32[128,32,128]{2,0,1:T(8,128)S(1)} %get-tuple-element.530, s32[68]{0:T(128)S(1)} %get-tuple-element.487, f32[68,128,128]{2,1,0:T(8,128)} %fusion.76), kind=kCustom, calls=%fused_computation.6.clone.1 | custom fusion | flops 1114112 | bytes 13369616 | tf_op jit(solution)/shard_map/while/body/eval_jaxpr/scatter-add | solution.py:34
  949.8 6.1 fusion.77
  955.8 10.5 %scatter_fusion.3 = f32[128,32,128]{2,0,1:T(8,128)S(1)} fusion(f32[128,32,128]{2,0,1:T(8,128)S(1)} %scatter_fusion.2, s32[68]{0:T(128)S(1)} %get-tuple-element.490, f32[68,128,128]{2,1,0:T(8,128)} %fusion.77), kind=kCustom, calls=%fused_computation.7.clone.1 | custom fusion | flops 1114112 | bytes 13369616 | tf_op jit(solution)/shard_map/while/body/eval_jaxpr/scatter-add | solution.py:34
  969.3 68.6 %reduce-scatter.2.cloned.1.call-done = f32[32,4096]{1,0:T(8,128)} async-done(((f32[128,4096]{1,0:T(8,128)}), f32[32,4096]{1,0:T(8,128)}) %reduce-scatter.2.cloned.1.call-update) | async-done | bytes 524304 | tf_op jit(solution)/shard_map/reduce_scatter | solution.py:95
  (148 shorter events, 148.6 us)
Async XLA Ops:
  7.2 283.8 %all-gather.6.cloned.1.call-start = ((), (), s32[]{:S(2)}) async-start(), calls=%async_computation.2 | async-start | bytes 1310720 | tf_op jit(solution)/shard_map/all_gather | solution.py:39
  7.9 292.9 %all-gather.8.cloned.1.call-start = ((), (), s32[]{:S(2)}) async-start(), calls=%async_computation.4 | async-start | bytes 18382848 | tf_op jit(solution)/shard_map/all_gather | solution.py:49
  16.0 8.9 copy-start.7
  16.0 10.1 copy-start.5
  16.0 10.2 copy-start.6
  16.0 273.7 %copy-start.4 = (bf16[128,3584]{1,0:T(8,128)(2,1)S(1)}, bf16[128,3584]{1,0:T(8,128)(2,1)}, u32[]{:S(2)}) copy-start(bf16[128,3584]{1,0:T(8,128)(2,1)} %param.19) | copy-start | bytes 2752516
  16.0 284.8 %all-to-all-start = ((bf16[32,17,128,128]{3,2,1,0:T(8,128)(2,1)}), bf16[32,17,128,128]{3,2,1,0:T(8,128)(2,1)}, u32[]{:S(2)}, u32[]{:S(2)}) async-start(bf16[32,17,128,128]{3,2,1,0:T(8,128)(2,1)} %stack.3), calls=%async_computation | async-start | bytes 35651584 | tf_op jit(solution)/shard_map/all_to_all | solution.py:10
  24.8 1013.1 %reduce-scatter.2.cloned.1.call-start = ((), (), s32[]{:S(2)}) async-start(), calls=%async_computation.3 | async-start | bytes 2621440 | tf_op jit(solution)/shard_map/reduce_scatter | solution.py:95
  640.9 2.9 copy-start
  640.9 2.9 copy-start.1
  647.9 1.7 copy-start.3
  966.4 1.6 copy-start.2
Sparse Core Ops, SparseCore 0:
  9.7 26.4 all-gather.5
  38.4 261.8 all-gather.7
  968.1 69.7 reduce-scatter.1
